TPU v7x, 32 devices: a whole 2x2x4 slice. The times are simulated.
32 devices in a mesh: sector: 4 (over z), axial: 8 (over y, x, core).
Axes of the slice: x: 2, y: 2, z: 4, core: 2. Of those that a mesh axis runs over, the one named last changes fastest.
Arguments:
- kbb: float32 [4096, 64, 64], P(('sector', 'axial')), as said below
- interior: bfloat16 [4096, 256, 64], P(('sector', 'axial')), may hold values from -0.075683594 to 0.075683594
- node_lists: int32 [4096, 64], P(('sector', 'axial')), may hold values from -1 to 63
- owners: int32 [4096, 1], P(('sector', 'axial')), may hold values from 0 to 31; in each aligned block of 128 rows (0 to 127, 128 to 255, ...) at most 8 rows name the same one
- patch_ids: int32 [4096], P(('sector', 'axial')), may hold values from 0 to 63
- counts: int32 [32], P(('sector', 'axial')), may hold values from 96 to 128
- capacity: float32 [131072], P(('sector', 'axial')), may hold values from 0.2 to 2
- links: int32 [2, 512, 2], P(None, ('sector', 'axial')), may hold values from 0 to 63
- conduct: float32 [2, 512, 64], P(None, ('sector', 'axial')), may hold values from 0.5 to 4
- loads: float32 [131072, 128], P(('sector', 'axial')), may hold values from -24 to 24
Outputs:
- current_estimate: float32 [131072, 128], P(('sector', 'axial'))
- remaining_imbalance: float32 [131072, 128], P(('sector', 'axial'))
Inputs may be any that keep to these rules, and one draw needn't show every extreme that they name: `owners`: no owner is named by more than 8 of one device's slots, live or not, and in every draw some owner is named by exactly 8 of some device's slots. The live slots of a device are its first counts slots; the others are padding. `kbb`: the boundary block is symmetric with non-positive entries off the diagonal whose row sums stay under its diagonal.
All inputs are finite; a program needn't handle non-finite values.
Results may differ from a plain program's by a relative error of at most 0.0003.
Values sent between devices are 32-bit elements; how exact they have to be, the bound alone decides.
No kernel may reach another device: no remote copies, remote signals or barrier semaphores. Data moves between devices by JAX's collectives and lax.ppermute only.
A program may use at most 128 MiB of HBM per device.

v0:
```python
import jax
import jax.numpy as jnp
from jax import lax
from jax.sharding import PartitionSpec as P

ITERS = 3
highest = lax.Precision.HIGHEST


def from_behind(array, axis, by):
    length = lax.axis_size(axis)
    return lax.ppermute(array, axis, [(i, (i + by) % length) for i in range(length)])


def shifted(block, axis, distance):
    devices = range(lax.axis_size(axis))
    route = [(i - distance, i) for i in devices if i - distance in devices]
    return lax.ppermute(block, axis, route)


def onehot_rows(index, count):
    return (index[:, None] == jnp.arange(count, dtype=jnp.int32)[None, :]).astype(jnp.float32)


def spread_field(index, values, count):
    return jnp.einsum("lp,lir->pir", onehot_rows(index, count), values, precision=highest)


def spread_flat(index, values, count):
    return jnp.einsum("lp,li->pi", onehot_rows(index, count), values, precision=highest)


def shards(kbb, interior, node_lists, owners, patch_ids, counts, capacity, links, conduct, loads):
    elem_slots, bound_nodes = node_lists.shape
    devices = lax.axis_size("sector") * lax.axis_size("axial")
    slots_each = 2 * elem_slots // devices
    total_slots = devices * slots_each
    points_in_partition, scenario_vectors = loads.shape
    patch_dev = points_in_partition // bound_nodes
    schur = kbb - jnp.einsum("eib,eic->ebc", interior, interior, preferred_element_type=jnp.float32)
    live = (jnp.arange(elem_slots, dtype=jnp.int32) < counts[0]).astype(jnp.int32)
    owner_hot = onehot_rows(owners[:, 0], devices)
    ranks = jnp.sum(jnp.cumsum(owner_hot, axis=0) * owner_hot, axis=1).astype(jnp.int32) - 1
    target = owners[:, 0] * slots_each + ranks
    send_blocks = (
        jnp.zeros((total_slots, bound_nodes, bound_nodes), jnp.float32).at[target].set(schur)
    )
    send_nodes = jnp.full((total_slots, bound_nodes), -1, jnp.int32).at[target].set(node_lists)
    send_patch = jnp.zeros((total_slots,), jnp.int32).at[target].set(patch_ids)
    send_live = jnp.zeros((total_slots,), jnp.int32).at[target].set(live)
    blocks_in, nodes_in, patch_in, live_in = (
        lax.all_to_all(send_blocks, ("sector", "axial"), split_axis=0, concat_axis=0, tiled=True),
        lax.all_to_all(send_nodes, ("sector", "axial"), split_axis=0, concat_axis=0, tiled=True),
        lax.all_to_all(send_patch, ("sector", "axial"), split_axis=0, concat_axis=0, tiled=True),
        lax.all_to_all(send_live, ("sector", "axial"), split_axis=0, concat_axis=0, tiled=True),
    )
    picker = (
        nodes_in[:, :, None] == jnp.arange(bound_nodes, dtype=jnp.int32)[None, None, :]
    ).astype(jnp.float32)
    half = jnp.einsum("rsj,rst->rjt", picker, blocks_in, precision=highest)
    placed = jnp.einsum("rjt,rtk->rjk", half, picker, precision=highest)
    weights = onehot_rows(patch_in, patch_dev) * live_in[:, None].astype(jnp.float32)
    assembled = jnp.einsum("rp,rjk->pjk", weights, placed, precision=highest)
    sector_own = links[0, :, 0]
    sector_far = links[0, :, 1]
    sector_gain = conduct[0]
    axial_own = links[1, :, 0]
    axial_far = links[1, :, 1]
    axial_gain = conduct[1]
    sector_in_far, sector_in_gain = from_behind((sector_far, sector_gain), "sector", 1)
    axial_in_far, axial_in_gain = shifted((axial_far, axial_gain), "axial", 1)
    heat = capacity.reshape(patch_dev, bound_nodes)
    diagonal = heat + jnp.diagonal(assembled, axis1=1, axis2=2)
    diagonal = (
        diagonal
        + spread_flat(sector_own, sector_gain, patch_dev)
        + spread_flat(sector_in_far, sector_in_gain, patch_dev)
    )
    diagonal = (
        diagonal
        + spread_flat(axial_own, axial_gain, patch_dev)
        + spread_flat(axial_in_far, axial_in_gain, patch_dev)
    )

    def precond_sum(remaining_imbalance, precond):
        return lax.psum(jnp.sum(remaining_imbalance * precond, axis=(0, 1)), ("sector", "axial"))

    remaining_imbalance = loads.reshape(patch_dev, bound_nodes, scenario_vectors)
    current_estimate = jnp.zeros_like(remaining_imbalance)
    scale = diagonal[:, :, None]
    precond = remaining_imbalance / scale
    update_vector = precond
    norm_now = precond_sum(remaining_imbalance, precond)
    for sweep in range(ITERS):
        result = heat[:, :, None] * update_vector + jnp.einsum(
            "pij,pjr->pir", assembled, update_vector, precision=highest
        )
        beyond = from_behind(update_vector[sector_in_far], "sector", -1)
        flux = sector_gain[:, :, None] * (update_vector[sector_own] - beyond)
        passed = from_behind(flux, "sector", 1)
        result = (
            result
            + spread_field(sector_own, flux, patch_dev)
            - spread_field(sector_in_far, passed, patch_dev)
        )
        beyond = shifted(update_vector[axial_in_far], "axial", -1)
        flux = axial_gain[:, :, None] * (update_vector[axial_own] - beyond)
        passed = shifted(flux, "axial", 1)
        result = (
            result
            + spread_field(axial_own, flux, patch_dev)
            - spread_field(axial_in_far, passed, patch_dev)
        )
        update_factor = norm_now / lax.psum(
            jnp.sum(update_vector * result, axis=(0, 1)), ("sector", "axial")
        )
        current_estimate = current_estimate + update_factor * update_vector
        remaining_imbalance = remaining_imbalance - update_factor * result
        if sweep + 1 < ITERS:
            precond = remaining_imbalance / scale
            norm_next = precond_sum(remaining_imbalance, precond)
            update_vector = precond + norm_next / norm_now * update_vector
            norm_now = norm_next
    return (
        current_estimate.reshape(points_in_partition, scenario_vectors),
        remaining_imbalance.reshape(points_in_partition, scenario_vectors),
    )


def solution(mesh):
    placed = (
        P(("sector", "axial"), None, None),
        P(("sector", "axial"), None, None),
        P(("sector", "axial"), None),
        P(("sector", "axial"), None),
        P(("sector", "axial")),
        P(("sector", "axial")),
        P(("sector", "axial")),
        P(None, ("sector", "axial"), None),
        P(None, ("sector", "axial"), None),
        P(("sector", "axial"), None),
    )
    return jax.shard_map(
        shards,
        mesh=mesh,
        in_specs=placed,
        out_specs=(P(("sector", "axial"), None), P(("sector", "axial"), None)),
        check_vma=False,
    )
```

profile of v0, /device:TPU:10, one launch (start us, length us, event | category | flops | bytes accessed | tf_op | source)
XLA Modules:
  0.0 622.8 jit_solution(7202846408577687185)
XLA Ops:
  5.4 6.0 all-to-all-start.1
  13.2 3.1 all-to-all-done.1
  16.4 4.6 all-to-all-start
  21.0 5.6 copy.75
  28.3 5.9 all-to-all-start.2
  34.2 7.9 %convolution_subtract_fusion = f32[128,64,64]{2,1,0:T(8,128)} fusion(f32[128,64,64]{2,1,0:T(8,128)} %copy.75, bf16[128,256,64]{1,2,0:T(8,128)(2,1)} %param.11), kind=kOutput, calls=%fused_computation.25 | convolution fusion | flops 268959744 | bytes 8388608 | tf_op jit(solution)/shard_map/eib,eic->ebc/dot_general | solution.py:40
  42.1 4.3 broadcast_in_dim.11
  46.4 19.3 %scatter_fusion = f32[256,64,64]{2,1,0:T(8,128)} fusion(f32[256,64,64]{2,1,0:T(8,128)} %broadcast_in_dim.11, s32[128]{0:T(128)S(1)} %fusion.85, f32[128,64,64]{2,1,0:T(8,128)} %convolution_subtract_fusion), kind=kCustom, calls=%fused_computation.16 | custom fusion | bytes 6291968 | tf_op jit(solution)/shard_map/scatter | solution.py:46
  65.7 9.8 %reshape.288 = f32[32,1,32768]{2,1,0:T(1,128)} reshape(f32[256,64,64]{2,1,0:T(8,128)} %scatter_fusion) | data formatting | bytes 8388608
  75.6 5.9 all-to-all-start.3
  86.5 3.5 collective-permute-start.2
  90.4 13.4 %collective-permute-done.2 = s32[16]{0:T(128)S(1)} collective-permute-done((s32[16]{0:T(128)S(1)}, s32[16]{0:T(128)S(1)}, u32[]{:S(2)}, u32[]{:S(2)}) %collective-permute-start.2) | collective-permute-done | bytes 96 | tf_op jit(solution)/shard_map/ppermute | solution.py:18
  106.6 65.6 %all-to-all-done.3 = f32[32,1,32768]{2,1,0:T(1,128)} async-done(((f32[32,1,32768]{2,1,0:T(1,128)}), f32[32,1,32768]{2,1,0:T(1,128)}, u32[]{:S(2)}, u32[]{:S(2)}) %all-to-all-start.3) | async-done | bytes 4194336 | tf_op jit(solution)/shard_map/all_to_all | solution.py:52
  172.7 13.7 %reduce.9 = f32[32,32768]{1,0:T(8,128)} reduce(f32[32,1,32768]{2,1,0:T(1,128)} %all-to-all-done.3, f32[]{:T(128)} %broadcast.166), dimensions={1}, to_apply=%all_to_all.27.reduce_sub_computation | reduce | bytes 8388612 | tf_op jit(solution)/shard_map/all_to_all | solution.py:52
  186.5 7.4 %reshape.289 = f32[256,64,64]{2,1,0:T(8,128)} reshape(f32[32,32768]{1,0:T(8,128)} %reduce.9) | data formatting | bytes 8388608
  193.8 11.8 %fusion.3 = f32[256,64,64]{2,1,0:T(8,128)S(1)} fusion(f32[256,64,64]{2,1,0:T(8,128)} %reshape.289, s32[256,64]{1,0:T(8,128)S(1)} %bitcast.83), kind=kOutput, calls=%fused_computation.21 | convolution fusion | flops 806354944 | bytes 8454144 | tf_op jit(solution)/shard_map/rsj,rst->rjt/dot_general | solution.py:60
  205.7 8.2 %fusion.2 = f32[256,64,64]{2,1,0:T(8,128)S(1)} fusion(f32[256,64,64]{2,1,0:T(8,128)S(1)} %fusion.3, s32[256,64]{1,0:T(8,128)S(1)} %bitcast.84), kind=kOutput, calls=%fused_computation.20 | convolution fusion | flops 806354944 | bytes 8454144 | tf_op jit(solution)/shard_map/rjt,rtk->rjk/dot_general | solution.py:61
  213.8 11.0 %fusion = f32[64,64,64]{2,0,1:T(8,128)} fusion(f32[256,64,64]{2,1,0:T(8,128)S(1)} %fusion.2, f32[256]{0:T(256)S(1)} %convert_element_type.50, s32[256]{0:T(256)S(1)} %eq.56), kind=kOutput, calls=%fused_computation.17 | convolution fusion | flops 805339136 | bytes 5244928 | tf_op jit(solution)/shard_map/rp,rjk->pjk/dot_general | solution.py:63
  224.9 3.0 copy.78
  232.2 3.0 gather_fusion.4
  235.1 2.8 collective-permute-start.6
  240.2 2.2 gather_fusion.1
  242.4 3.0 gather_fusion.2
  245.4 2.6 collective-permute-start.4
  252.1 8.1 %collective-permute-done.4 = f32[16,64,128]{2,1,0:T(8,128)S(1)} collective-permute-done((f32[16,64,128]{2,1,0:T(8,128)}, f32[16,64,128]{2,1,0:T(8,128)S(1)}, u32[]{:S(2)}, u32[]{:S(2)}) %collective-permute-start.4) | collective-permute-done | bytes 524320 | tf_op jit(solution)/shard_map/ppermute | solution.py:12
  265.6 9.5 %collective-permute-done.5 = f32[16,64,128]{2,1,0:T(8,128)S(1)} collective-permute-done((f32[16,64,128]{2,1,0:T(8,128)S(1)}, f32[16,64,128]{2,1,0:T(8,128)S(1)}, u32[]{:S(2)}, u32[]{:S(2)}) %collective-permute-start.5) | collective-permute-done | bytes 524320 | tf_op jit(solution)/shard_map/ppermute | solution.py:12
  276.2 13.9 %multiply_reduce_fusion.4 = (f32[128]{0:T(128)S(1)}, f32[64,64,128]{2,1,0:T(8,128)}) fusion(f32[64,64,128]{2,1,0:T(8,128)S(1)} %copy-done.6, f32[64,64,128]{2,0,1:T(8,128)S(1)} %fusion.36, f32[64,64,128]{2,0,1:T(8,128)S(1)} %fusion.38, f32[64,64,128]{2,0,1:T(8,128)S(1)} %fusion.40, f32[64,64,128]{2,0,1:T(8,128)S(1)} %fusion.42, ...), kind=kOutput, calls=%fused_computation.48 | convolution fusion | flops 406847360 | bytes 13648384 | tf_op jit(solution)/shard_map/pij,pjr->pir/dot_general | solution.py:95
  290.1 43.9 %all-reduce = (f32[128]{0:T(128)S(1)}, f32[128]{0:T(128)S(1)}) all-reduce(f32[128]{0:T(128)S(1)} %fusion.6, f32[128]{0:T(128)S(1)} %get-tuple-element.18), channel_id=1, replica_groups=mesh['sector'=4,'axial'=8] {'sector','axial'}, use_global_device_ids=true, to_apply=%region_7.8 | all-reduce | flops 256 | bytes 2048 | tf_op jit(solution)/shard_map/psum | solution.py:86
  334.1 2.9 multiply_reduce_fusion.3
  336.9 38.0 %psum.44 = f32[128]{0:T(128)S(1)} all-reduce(f32[128]{0:T(128)S(1)} %get-tuple-element.6), channel_id=1, replica_groups=mesh['sector'=4,'axial'=8] {'sector','axial'}, use_global_device_ids=true, to_apply=%region_11.12 | all-reduce | flops 128 | bytes 1024 | tf_op jit(solution)/shard_map/psum | solution.py:86
  374.9 3.1 multiply_add_fusion.2
  378.0 3.0 gather_fusion.8
  382.9 3.0 gather_fusion.6
  390.1 2.2 gather_fusion.5
  395.7 4.8 collective-permute-done.8
  406.4 9.3 %collective-permute-done.9 = f32[16,64,128]{2,1,0:T(8,128)S(1)} collective-permute-done((f32[16,64,128]{2,1,0:T(8,128)S(1)}, f32[16,64,128]{2,1,0:T(8,128)S(1)}, u32[]{:S(2)}, u32[]{:S(2)}) %collective-permute-start.9) | collective-permute-done | bytes 524320 | tf_op jit(solution)/shard_map/ppermute | solution.py:12
  416.9 13.9 %multiply_reduce_fusion.2 = (f32[128]{0:T(128)S(1)}, f32[64,64,128]{2,1,0:T(8,128)}) fusion(f32[64,64,128]{2,1,0:T(8,128)S(1)} %copy-done.1, f32[64,64,128]{2,0,1:T(8,128)S(1)} %fusion.28, f32[64,64,128]{2,0,1:T(8,128)S(1)} %fusion.30, f32[64,64,128]{2,0,1:T(8,128)S(1)} %fusion.32, f32[64,64,128]{2,0,1:T(8,128)S(1)} %fusion.34, ...), kind=kOutput, calls=%fused_computation.44 | convolution fusion | flops 406847360 | bytes 13648384 | tf_op jit(solution)/shard_map/pij,pjr->pir/dot_general | solution.py:95
  430.8 44.4 %psum.45 = f32[128]{0:T(128)S(1)} all-reduce(f32[128]{0:T(128)S(1)} %get-tuple-element.20), channel_id=1, replica_groups=mesh['sector'=4,'axial'=8] {'sector','axial'}, use_global_device_ids=true, to_apply=%region_13.14 | all-reduce | flops 128 | bytes 1024 | tf_op jit(solution)/shard_map/psum | solution.py:114
  475.1 3.5 multiply_reduce_fusion.1
  478.6 38.0 %psum.46 = f32[128]{0:T(128)S(1)} all-reduce(f32[128]{0:T(128)S(1)} %get-tuple-element.4), channel_id=1, replica_groups=mesh['sector'=4,'axial'=8] {'sector','axial'}, use_global_device_ids=true, to_apply=%region_15.16 | all-reduce | flops 128 | bytes 1024 | tf_op jit(solution)/shard_map/psum | solution.py:86
  516.6 3.6 multiply_add_fusion.1
  520.1 3.0 gather_fusion.12
  525.0 3.0 gather_fusion.10
  537.9 4.8 collective-permute-done.12
  548.6 9.3 %collective-permute-done.13 = f32[16,64,128]{2,1,0:T(8,128)S(1)} collective-permute-done((f32[16,64,128]{2,1,0:T(8,128)S(1)}, f32[16,64,128]{2,1,0:T(8,128)S(1)}, u32[]{:S(2)}, u32[]{:S(2)}) %collective-permute-start.13) | collective-permute-done | bytes 524320 | tf_op jit(solution)/shard_map/ppermute | solution.py:12
  559.0 13.9 %multiply_reduce_fusion = (f32[128]{0:T(128)S(1)}, f32[64,64,128]{2,1,0:T(8,128)}) fusion(f32[64,64,128]{2,1,0:T(8,128)S(1)} %copy-done.5, f32[64,64,128]{2,0,1:T(8,128)S(1)} %fusion.20, f32[64,64,128]{2,0,1:T(8,128)S(1)} %fusion.22, f32[64,64,128]{2,0,1:T(8,128)S(1)} %fusion.24, f32[64,64,128]{2,0,1:T(8,128)S(1)} %fusion.26, ...), kind=kOutput, calls=%fused_computation.40 | convolution fusion | flops 406847360 | bytes 13648384 | tf_op jit(solution)/shard_map/pij,pjr->pir/dot_general | solution.py:95
  572.9 44.1 %psum.47 = f32[128]{0:T(128)S(1)} all-reduce(f32[128]{0:T(128)S(1)} %get-tuple-element.22), channel_id=1, replica_groups=mesh['sector'=4,'axial'=8] {'sector','axial'}, use_global_device_ids=true, to_apply=%region_17.18 | all-reduce | flops 128 | bytes 1024 | tf_op jit(solution)/shard_map/psum | solution.py:114
  617.1 5.3 multiply_subtract_fusion
  (114 shorter events, 68.8 us)
Async XLA Ops:
  5.4 11.0 %all-to-all-start.1 = ((s32[32,8,1]{1,2,0:T(1,128)}), s32[32,8,1]{1,2,0:T(1,128)S(1)}, u32[]{:S(2)}, u32[]{:S(2)}) async-start(s32[32,8,1]{1,2,0:T(1,128)} %bitcast.5), calls=%async_computation.1 | async-start | bytes 32768 | tf_op jit(solution)/shard_map/all_to_all | solution.py:55
  16.4 12.0 %all-to-all-start = ((s32[32,8,1]{1,2,0:T(1,128)}), s32[32,8,1]{1,2,0:T(1,128)S(1)}, u32[]{:S(2)}, u32[]{:S(2)}) async-start(s32[32,8,1]{1,2,0:T(1,128)} %bitcast.3), calls=%async_computation | async-start | bytes 32768 | tf_op jit(solution)/shard_map/all_to_all | solution.py:54
  21.0 5.6 copy-start.8
  28.3 47.2 %all-to-all-start.2 = ((s32[32,1,512]{2,1,0:T(1,128)}), s32[32,1,512]{2,1,0:T(1,128)S(1)}, u32[]{:S(2)}, u32[]{:S(2)}) async-start(s32[32,1,512]{2,1,0:T(1,128)} %reshape.290), calls=%async_computation.2 | async-start | bytes 131072 | tf_op jit(solution)/shard_map/all_to_all | solution.py:53
  75.5 5.9 copy-start.7
  75.5 7.5 %copy-start.10 = (s32[2,16,2]{1,2,0:T(2,128)S(1)}, s32[2,16,2]{1,2,0:T(2,128)}, u32[]{:S(2)}) copy-start(s32[2,16,2]{1,2,0:T(2,128)} %param.17) | copy-start | bytes 772
  75.5 14.8 %copy-start.9 = (f32[4096]{0:T(1024)S(1)}, f32[4096]{0:T(1024)}, u32[]{:S(2)}) copy-start(f32[4096]{0:T(1024)} %param.16) | copy-start | bytes 49156
  75.6 96.7 %all-to-all-start.3 = ((f32[32,1,32768]{2,1,0:T(1,128)}), f32[32,1,32768]{2,1,0:T(1,128)}, u32[]{:S(2)}, u32[]{:S(2)}) async-start(f32[32,1,32768]{2,1,0:T(1,128)} %reshape.288), calls=%async_computation.3 | async-start | bytes 8388608 | tf_op jit(solution)/shard_map/all_to_all | solution.py:52
  81.5 148.4 %collective-permute-start.1 = (f32[16,64]{1,0:T(8,128)S(1)}, f32[16,64]{1,0:T(8,128)S(1)}, u32[]{:S(2)}, u32[]{:S(2)}) collective-permute-start(f32[16,64]{1,0:T(8,128)S(1)} %get-tuple-element.9), channel_id=1, source_target_pairs={{0,8},{8,16},{16,24},{24,0},{1,9},{9,17},{17,25},{25,1},{2,10},{10... | collective-permute-start | bytes 12296 | tf_op jit(solution)/shard_map/ppermute | solution.py:12
  83.0 146.8 %collective-permute-start = (s32[16]{0:T(128)S(1)}, s32[16]{0:T(128)S(1)}, u32[]{:S(2)}, u32[]{:S(2)}) collective-permute-start(s32[16]{0:T(128)S(1)} %get-tuple-element.13), channel_id=1, source_target_pairs={{0,8},{8,16},{16,24},{24,0},{1,9},{9,17},{17,25},{25,1},{2,10},{10... | collective-permute-start | bytes 200 | tf_op jit(solution)/shard_map/ppermute | solution.py:12
  84.6 145.6 %collective-permute-start.3 = (f32[16,64]{1,0:T(8,128)S(1)}, f32[16,64]{1,0:T(8,128)S(1)}, u32[]{:S(2)}, u32[]{:S(2)}) collective-permute-start(f32[16,64]{1,0:T(8,128)S(1)} %get-tuple-element.8), channel_id=1, source_target_pairs={{0,1},{1,2},{2,3},{3,4},{4,5},{5,6},{6,7},{8,9},{9,10},{10,11},{11... | collective-permute-start | bytes 12296 | tf_op jit(solution)/shard_map/ppermute | solution.py:18
  86.5 17.3 %collective-permute-start.2 = (s32[16]{0:T(128)S(1)}, s32[16]{0:T(128)S(1)}, u32[]{:S(2)}, u32[]{:S(2)}) collective-permute-start(s32[16]{0:T(128)S(1)} %get-tuple-element.12), channel_id=1, source_target_pairs={{0,1},{1,2},{2,3},{3,4},{4,5},{5,6},{6,7},{8,9},{9,10},{10,11},{11... | collective-permute-start | bytes 200 | tf_op jit(solution)/shard_map/ppermute | solution.py:18
  224.9 5.6 copy-start
  235.1 13.5 %collective-permute-start.6 = (f32[16,64,128]{2,1,0:T(8,128)}, f32[16,64,128]{2,1,0:T(8,128)}, u32[]{:S(2)}, u32[]{:S(2)}) collective-permute-start(f32[16,64,128]{2,1,0:T(8,128)} %gather_fusion.4), channel_id=1, source_target_pairs={{1,0},{2,1},{3,2},{4,3},{5,4},{6,5},{7,6},{9,8},{10,9},{11,10},{12... | collective-permute-start | bytes 1572872 | tf_op jit(solution)/shard_map/ppermute | solution.py:18
  245.4 14.7 %collective-permute-start.4 = (f32[16,64,128]{2,1,0:T(8,128)}, f32[16,64,128]{2,1,0:T(8,128)S(1)}, u32[]{:S(2)}, u32[]{:S(2)}) collective-permute-start(f32[16,64,128]{2,1,0:T(8,128)} %gather_fusion.2), channel_id=1, source_target_pairs={{0,24},{8,0},{16,8},{24,16},{1,25},{9,1},{17,9},{25,17},{2,26},{10... | collective-permute-start | bytes 1572872 | tf_op jit(solution)/shard_map/ppermute | solution.py:12
  249.9 14.5 %collective-permute-start.7 = (f32[16,64,128]{2,1,0:T(8,128)S(1)}, f32[16,64,128]{2,1,0:T(8,128)S(1)}, u32[]{:S(2)}, u32[]{:S(2)}) collective-permute-start(f32[16,64,128]{2,1,0:T(8,128)S(1)} %subtract_multiply_fusion.4), channel_id=1, source_target_pairs={{0,1},{1,2},{2,3},{3,4},{4,5},{5,6},{6,7},{8,9},{9,10},{10,11},{11... | collective-permute-start | bytes 1572872 | tf_op jit(solution)/shard_map/ppermute | solution.py:18
  260.4 14.7 %collective-permute-start.5 = (f32[16,64,128]{2,1,0:T(8,128)S(1)}, f32[16,64,128]{2,1,0:T(8,128)S(1)}, u32[]{:S(2)}, u32[]{:S(2)}) collective-permute-start(f32[16,64,128]{2,1,0:T(8,128)S(1)} %subtract_multiply_fusion.5), channel_id=1, source_target_pairs={{0,8},{8,16},{16,24},{24,0},{1,9},{9,17},{17,25},{25,1},{2,10},{10... | collective-permute-start | bytes 1572872 | tf_op jit(solution)/shard_map/ppermute | solution.py:12
  264.4 11.9 %copy-start.2 = (f32[64,64,64]{2,0,1:T(8,128)S(1)}, f32[64,64,64]{2,0,1:T(8,128)}, u32[]{:S(2)}) copy-start(f32[64,64,64]{2,0,1:T(8,128)} %fusion) | copy-start | bytes 3145732
  264.4 11.9 %copy-start.6 = (f32[64,64,128]{2,1,0:T(8,128)S(1)}, f32[64,64,128]{2,1,0:T(8,128)}, u32[]{:S(2)}) copy-start(f32[64,64,128]{2,1,0:T(8,128)} %broadcast_divide_fusion) | copy-start | bytes 6291460
  381.0 11.3 %collective-permute-start.10 = (f32[16,64,128]{2,1,0:T(8,128)}, f32[16,64,128]{2,1,0:T(8,128)}, u32[]{:S(2)}, u32[]{:S(2)}) collective-permute-start(f32[16,64,128]{2,1,0:T(8,128)} %gather_fusion.8), channel_id=1, source_target_pairs={{1,0},{2,1},{3,2},{4,3},{5,4},{6,5},{7,6},{9,8},{10,9},{11,10},{12... | collective-permute-start | bytes 1572872 | tf_op jit(solution)/shard_map/ppermute | solution.py:18
  385.8 14.6 %collective-permute-start.8 = (f32[16,64,128]{2,1,0:T(8,128)}, f32[16,64,128]{2,1,0:T(8,128)}, u32[]{:S(2)}, u32[]{:S(2)}) collective-permute-start(f32[16,64,128]{2,1,0:T(8,128)} %gather_fusion.6), channel_id=1, source_target_pairs={{0,24},{8,0},{16,8},{24,16},{1,25},{9,1},{17,9},{25,17},{2,26},{10... | collective-permute-start | bytes 1572872 | tf_op jit(solution)/shard_map/ppermute | solution.py:12
  393.5 11.7 %collective-permute-start.11 = (f32[16,64,128]{2,1,0:T(8,128)S(1)}, f32[16,64,128]{2,1,0:T(8,128)S(1)}, u32[]{:S(2)}, u32[]{:S(2)}) collective-permute-start(f32[16,64,128]{2,1,0:T(8,128)S(1)} %subtract_multiply_fusion.2), channel_id=1, source_target_pairs={{0,1},{1,2},{2,3},{3,4},{4,5},{5,6},{6,7},{8,9},{9,10},{10,11},{11... | collective-permute-start | bytes 1572872 | tf_op jit(solution)/shard_map/ppermute | solution.py:18
  401.7 14.0 %collective-permute-start.9 = (f32[16,64,128]{2,1,0:T(8,128)S(1)}, f32[16,64,128]{2,1,0:T(8,128)S(1)}, u32[]{:S(2)}, u32[]{:S(2)}) collective-permute-start(f32[16,64,128]{2,1,0:T(8,128)S(1)} %subtract_multiply_fusion.3), channel_id=1, source_target_pairs={{0,8},{8,16},{16,24},{24,0},{1,9},{9,17},{17,25},{25,1},{2,10},{10... | collective-permute-start | bytes 1572872 | tf_op jit(solution)/shard_map/ppermute | solution.py:12
  405.2 11.7 %copy-start.1 = (f32[64,64,128]{2,1,0:T(8,128)S(1)}, f32[64,64,128]{2,1,0:T(8,128)}, u32[]{:S(2)}) copy-start(f32[64,64,128]{2,1,0:T(8,128)} %multiply_add_fusion.2) | copy-start | bytes 6291460
  405.2 11.7 %copy-start.3 = (f32[64,64,64]{2,0,1:T(8,128)S(1)}, f32[64,64,64]{2,0,1:T(8,128)}, u32[]{:S(2)}) copy-start(f32[64,64,64]{2,0,1:T(8,128)} %fusion) | copy-start | bytes 3145732
  523.1 11.4 %collective-permute-start.14 = (f32[16,64,128]{2,1,0:T(8,128)}, f32[16,64,128]{2,1,0:T(8,128)}, u32[]{:S(2)}, u32[]{:S(2)}) collective-permute-start(f32[16,64,128]{2,1,0:T(8,128)} %gather_fusion.12), channel_id=1, source_target_pairs={{1,0},{2,1},{3,2},{4,3},{5,4},{6,5},{7,6},{9,8},{10,9},{11,10},{12... | collective-permute-start | bytes 1572872 | tf_op jit(solution)/shard_map/ppermute | solution.py:18
  528.0 14.6 %collective-permute-start.12 = (f32[16,64,128]{2,1,0:T(8,128)}, f32[16,64,128]{2,1,0:T(8,128)}, u32[]{:S(2)}, u32[]{:S(2)}) collective-permute-start(f32[16,64,128]{2,1,0:T(8,128)} %gather_fusion.10), channel_id=1, source_target_pairs={{0,24},{8,0},{16,8},{24,16},{1,25},{9,1},{17,9},{25,17},{2,26},{10... | collective-permute-start | bytes 1572872 | tf_op jit(solution)/shard_map/ppermute | solution.py:12
  535.7 11.7 %collective-permute-start.15 = (f32[16,64,128]{2,1,0:T(8,128)S(1)}, f32[16,64,128]{2,1,0:T(8,128)S(1)}, u32[]{:S(2)}, u32[]{:S(2)}) collective-permute-start(f32[16,64,128]{2,1,0:T(8,128)S(1)} %subtract_multiply_fusion), channel_id=1, source_target_pairs={{0,1},{1,2},{2,3},{3,4},{4,5},{5,6},{6,7},{8,9},{9,10},{10,11},{11... | collective-permute-start | bytes 1572872 | tf_op jit(solution)/shard_map/ppermute | solution.py:18
  543.9 14.0 %collective-permute-start.13 = (f32[16,64,128]{2,1,0:T(8,128)S(1)}, f32[16,64,128]{2,1,0:T(8,128)S(1)}, u32[]{:S(2)}, u32[]{:S(2)}) collective-permute-start(f32[16,64,128]{2,1,0:T(8,128)S(1)} %subtract_multiply_fusion.1), channel_id=1, source_target_pairs={{0,8},{8,16},{16,24},{24,0},{1,9},{9,17},{17,25},{25,1},{2,10},{10... | collective-permute-start | bytes 1572872 | tf_op jit(solution)/shard_map/ppermute | solution.py:12
  547.4 11.6 %copy-start.4 = (f32[64,64,64]{2,0,1:T(8,128)S(1)}, f32[64,64,64]{2,0,1:T(8,128)}, u32[]{:S(2)}) copy-start(f32[64,64,64]{2,0,1:T(8,128)} %fusion) | copy-start | bytes 3145732
  547.4 11.6 %copy-start.5 = (f32[64,64,128]{2,1,0:T(8,128)S(1)}, f32[64,64,128]{2,1,0:T(8,128)}, u32[]{:S(2)}) copy-start(f32[64,64,128]{2,1,0:T(8,128)} %multiply_add_fusion.1) | copy-start | bytes 6291460
where the time goes:
time: 633 us; the launch traced here: 623 us
  blocking collectives  208 us (33%)
  waiting for transfers between devices  128 us (20%)
  matrix products  95.7 us (15%)
  local copies, waits for them, and re-layouts  89.1 us (14%)
  starting transfers between devices  54.6 us (9%)
  other arithmetic  44.9 us (7%)
    psum x3, blocking collectives, precond_sum(): lax.psum(jnp.sum(remaining_imbalance * precond, axis=(0, 1)), ('sector',...  120 us
    psum x2, blocking collectives, shards(): lax.psum(jnp.sum(update_vector * result, axis=(0, 1)), ('sector', 'axial'))  88.5 us
    all_to_all x1, waiting for transfers between devices, shards(): lax.all_to_all(send_blocks, ('sector', 'axial'), split_axis=0, concat_axi...  65.6 us
    ppermute x8, waiting for transfers between devices, from_behind(): lax.ppermute(array, axis, [(i, (i + by) % length) for i in range(length)])  45.7 us
    dot_general x3, matrix products, shards(): jnp.einsum('pij,pjr->pir', assembled, update_vector, precision=highest)  41.7 us
    unnamed x28, local copies, waits for them, and re-layouts  23.7 us
    scatter x1, local copies, waits for them, and re-layouts, shards(): jnp.zeros((total_slots, bound_nodes, bound_nodes), jnp.float32).at[target]  19.3 us
    ppermute x8, starting transfers between devices, shifted(): return lax.ppermute(block, axis, route)  18.4 us
  transfers between devices with their start and end apart: 20, of which 9 were waited for; matrix products, arithmetic and copies ran while one was open for 24% of the time, Pallas kernels for 0%

commit v1 on v0

--- a/solution.py
+++ b/solution.py
@@ -83,7 +83,12 @@
     )
 
     def precond_sum(remaining_imbalance, precond):
-        return lax.psum(jnp.sum(remaining_imbalance * precond, axis=(0, 1)), ("sector", "axial"))
+        return jnp.sum(
+            lax.all_gather(
+                jnp.sum(remaining_imbalance * precond, axis=(0, 1)), ("sector", "axial")
+            ),
+            axis=0,
+        )
 
     remaining_imbalance = loads.reshape(patch_dev, bound_nodes, scenario_vectors)
     current_estimate = jnp.zeros_like(remaining_imbalance)

time: 633 us -> 661 us (1.044)
  blocking collectives: 208 us -> 236 us
  waiting for transfers between devices: 128 us -> 116 us
  starting transfers between devices: 54.6 us -> 66.2 us
    psum x3 -> x0, blocking collectives: 120 us -> none  [precond_sum(): lax.psum(jnp.sum(remaining_imbalance * precond, axis=(0, 1)), ('sector',...]
    all_gather x0 -> x3, blocking collectives: none -> 96.3 us  [precond_sum(): lax.all_gather(jnp.sum(remaining_imbalance * precond, axis=(0, 1)), ('sec...]
    psum x2 -> x3, blocking collectives: 88.5 us -> 140 us  [shards(): lax.psum(jnp.sum(update_vector * result, axis=(0, 1)), ('sector', 'axial'))]
    ppermute x8, waiting for transfers between devices: 45.7 us -> 22.1 us  [from_behind(): lax.ppermute(array, axis, [(i, (i + by) % length) for i in range(length)])]
    ppermute x8, waiting for transfers between devices: 13.4 us -> 25.1 us  [shifted(): return lax.ppermute(block, axis, route)]
  transfers between devices with their start and end apart: 20 -> 20, of which waited for: 9 -> 11; matrix products, arithmetic and copies ran while one was open for 24% -> 23% of each run, Pallas kernels for 0% -> 0%
where the time goes in v1:
time: 661 us; the launch traced here: 651 us
  blocking collectives  236 us (36%)
  waiting for transfers between devices  116 us (18%)
  matrix products  95.7 us (14%)
  local copies, waits for them, and re-layouts  89.1 us (13%)
  starting transfers between devices  66.2 us (10%)
  other arithmetic  45.9 us (7%)
    psum x3, blocking collectives, shards(): lax.psum(jnp.sum(update_vector * result, axis=(0, 1)), ('sector', 'axial'))  140 us
    all_gather x3, blocking collectives, precond_sum(): lax.all_gather(jnp.sum(remaining_imbalance * precond, axis=(0, 1)), ('sec...  96.3 us
    all_to_all x1, waiting for transfers between devices, shards(): lax.all_to_all(send_blocks, ('sector', 'axial'), split_axis=0, concat_axi...  65.6 us
    dot_general x3, matrix products, shards(): jnp.einsum('pij,pjr->pir', assembled, update_vector, precision=highest)  41.7 us
    ppermute x8, waiting for transfers between devices, shifted(): return lax.ppermute(block, axis, route)  25.1 us
    ppermute x8, starting transfers between devices, shifted(): return lax.ppermute(block, axis, route)  23.8 us
    unnamed x28, local copies, waits for them, and re-layouts  23.7 us
    ppermute x8, waiting for transfers between devices, from_behind(): lax.ppermute(array, axis, [(i, (i + by) % length) for i in range(length)])  22.1 us
  transfers between devices with their start and end apart: 20, of which 11 were waited for; matrix products, arithmetic and copies ran while one was open for 23% of the time, Pallas kernels for 0%

profile of v1, /device:TPU:10, one launch (start us, length us, event | category | flops | bytes accessed | tf_op | source)
XLA Modules:
  0.0 651.1 jit_solution(9817096740255314056)
XLA Ops:
  5.4 6.0 all-to-all-start.1
  13.2 3.1 all-to-all-done.1
  16.4 4.6 all-to-all-start
  21.0 5.6 copy.75
  28.3 5.9 all-to-all-start.2
  34.2 7.9 %convolution_subtract_fusion = f32[128,64,64]{2,1,0:T(8,128)} fusion(f32[128,64,64]{2,1,0:T(8,128)} %copy.75, bf16[128,256,64]{1,2,0:T(8,128)(2,1)} %param.11), kind=kOutput, calls=%fused_computation.25 | convolution fusion | flops 268959744 | bytes 8388608 | tf_op jit(solution)/shard_map/eib,eic->ebc/dot_general | solution.py:40
  42.1 4.3 broadcast_in_dim.11
  46.4 19.3 %scatter_fusion = f32[256,64,64]{2,1,0:T(8,128)} fusion(f32[256,64,64]{2,1,0:T(8,128)} %broadcast_in_dim.11, s32[128]{0:T(128)S(1)} %fusion.85, f32[128,64,64]{2,1,0:T(8,128)} %convolution_subtract_fusion), kind=kCustom, calls=%fused_computation.16 | custom fusion | bytes 6291968 | tf_op jit(solution)/shard_map/scatter | solution.py:46
  65.7 9.8 %reshape.308 = f32[32,1,32768]{2,1,0:T(1,128)} reshape(f32[256,64,64]{2,1,0:T(8,128)} %scatter_fusion) | data formatting | bytes 8388608
  75.6 5.9 all-to-all-start.3
  86.5 3.5 collective-permute-start.2
  90.4 13.4 %collective-permute-done.2 = s32[16]{0:T(128)S(1)} collective-permute-done((s32[16]{0:T(128)S(1)}, s32[16]{0:T(128)S(1)}, u32[]{:S(2)}, u32[]{:S(2)}) %collective-permute-start.2) | collective-permute-done | bytes 96 | tf_op jit(solution)/shard_map/ppermute | solution.py:18
  106.6 65.6 %all-to-all-done.3 = f32[32,1,32768]{2,1,0:T(1,128)} async-done(((f32[32,1,32768]{2,1,0:T(1,128)}), f32[32,1,32768]{2,1,0:T(1,128)}, u32[]{:S(2)}, u32[]{:S(2)}) %all-to-all-start.3) | async-done | bytes 4194336 | tf_op jit(solution)/shard_map/all_to_all | solution.py:52
  172.7 13.7 %reduce.12 = f32[32,32768]{1,0:T(8,128)} reduce(f32[32,1,32768]{2,1,0:T(1,128)} %all-to-all-done.3, f32[]{:T(128)} %broadcast.164), dimensions={1}, to_apply=%all_to_all.27.reduce_sub_computation | reduce | bytes 8388612 | tf_op jit(solution)/shard_map/all_to_all | solution.py:52
  186.5 7.4 %reshape.309 = f32[256,64,64]{2,1,0:T(8,128)} reshape(f32[32,32768]{1,0:T(8,128)} %reduce.12) | data formatting | bytes 8388608
  193.8 11.8 %fusion.3 = f32[256,64,64]{2,1,0:T(8,128)S(1)} fusion(f32[256,64,64]{2,1,0:T(8,128)} %reshape.309, s32[256,64]{1,0:T(8,128)S(1)} %bitcast.86), kind=kOutput, calls=%fused_computation.21 | convolution fusion | flops 806354944 | bytes 8454144 | tf_op jit(solution)/shard_map/rsj,rst->rjt/dot_general | solution.py:60
  205.7 8.2 %fusion.2 = f32[256,64,64]{2,1,0:T(8,128)S(1)} fusion(f32[256,64,64]{2,1,0:T(8,128)S(1)} %fusion.3, s32[256,64]{1,0:T(8,128)S(1)} %bitcast.87), kind=kOutput, calls=%fused_computation.20 | convolution fusion | flops 806354944 | bytes 8454144 | tf_op jit(solution)/shard_map/rjt,rtk->rjk/dot_general | solution.py:61
  213.8 11.0 %fusion = f32[64,64,64]{2,0,1:T(8,128)} fusion(f32[256,64,64]{2,1,0:T(8,128)S(1)} %fusion.2, f32[256]{0:T(256)S(1)} %convert_element_type.50, s32[256]{0:T(256)S(1)} %eq.56), kind=kOutput, calls=%fused_computation.17 | convolution fusion | flops 805339136 | bytes 5244928 | tf_op jit(solution)/shard_map/rp,rjk->pjk/dot_general | solution.py:63
  224.9 3.0 copy.78
  232.2 3.0 gather_fusion.4
  242.4 3.0 gather_fusion.2
  248.7 39.1 %all-gather.3 = f32[32,1,128]{2,1,0:T(1,128)S(1)} all-gather(f32[1,1,128]{2,1,0:T(1,128)S(1)} %bitcast.91), channel_id=2, replica_groups=mesh['sector'=4,'axial'=8] {'sector','axial'}, dimensions={0}, use_global_device_ids=true | all-gather | bytes 16896 | tf_op jit(solution)/shard_map/all_gather | solution.py:87
  295.4 4.5 collective-permute-done.7
  301.0 9.7 %collective-permute-done.5 = f32[16,64,128]{2,1,0:T(8,128)S(1)} collective-permute-done((f32[16,64,128]{2,1,0:T(8,128)S(1)}, f32[16,64,128]{2,1,0:T(8,128)S(1)}, u32[]{:S(2)}, u32[]{:S(2)}) %collective-permute-start.5) | collective-permute-done | bytes 524320 | tf_op jit(solution)/shard_map/ppermute | solution.py:12
  311.9 13.9 %multiply_reduce_fusion.4 = (f32[128]{0:T(128)S(1)}, f32[64,64,128]{2,1,0:T(8,128)}) fusion(f32[64,64,128]{2,1,0:T(8,128)S(1)} %copy-done.6, f32[64,64,128]{2,0,1:T(8,128)S(1)} %fusion.36, f32[64,64,128]{2,0,1:T(8,128)S(1)} %fusion.38, f32[64,64,128]{2,0,1:T(8,128)S(1)} %fusion.40, f32[64,64,128]{2,0,1:T(8,128)S(1)} %fusion.42, ...), kind=kOutput, calls=%fused_computation.48 | convolution fusion | flops 406847360 | bytes 13648384 | tf_op jit(solution)/shard_map/pij,pjr->pir/dot_general | solution.py:100
  325.8 45.0 %psum.21 = f32[128]{0:T(128)S(1)} all-reduce(f32[128]{0:T(128)S(1)} %get-tuple-element.16), channel_id=1, replica_groups=mesh['sector'=4,'axial'=8] {'sector','axial'}, use_global_device_ids=true, to_apply=%region_9.10 | all-reduce | flops 128 | bytes 1024 | tf_op jit(solution)/shard_map/psum | solution.py:119
  373.7 28.6 %all-gather.4 = f32[32,1,128]{2,1,0:T(1,128)S(1)} all-gather(f32[1,1,128]{2,1,0:T(1,128)S(1)} %bitcast.93), channel_id=3, replica_groups=mesh['sector'=4,'axial'=8] {'sector','axial'}, dimensions={0}, use_global_device_ids=true | all-gather | bytes 16896 | tf_op jit(solution)/shard_map/all_gather | solution.py:87
  402.4 3.0 multiply_add_fusion.2
  405.4 3.0 gather_fusion.8
  408.3 4.8 collective-permute-start.10
  413.1 3.0 gather_fusion.6
  416.1 6.9 %collective-permute-start.8 = (f32[16,64,128]{2,1,0:T(8,128)}, f32[16,64,128]{2,1,0:T(8,128)}, u32[]{:S(2)}, u32[]{:S(2)}) collective-permute-start(f32[16,64,128]{2,1,0:T(8,128)} %gather_fusion.6), channel_id=1, source_target_pairs={{0,24},{8,0},{16,8},{24,16},{1,25},{9,1},{17,9},{25,17},{2,26},{10... | collective-permute-start | bytes 1572872 | tf_op jit(solution)/shard_map/ppermute | solution.py:12
  435.4 3.6 collective-permute-done.11
  440.2 5.0 collective-permute-done.9
  446.3 13.9 %multiply_reduce_fusion.2 = (f32[128]{0:T(128)S(1)}, f32[64,64,128]{2,1,0:T(8,128)}) fusion(f32[64,64,128]{2,1,0:T(8,128)S(1)} %copy-done.1, f32[64,64,128]{2,0,1:T(8,128)S(1)} %fusion.28, f32[64,64,128]{2,0,1:T(8,128)S(1)} %fusion.30, f32[64,64,128]{2,0,1:T(8,128)S(1)} %fusion.32, f32[64,64,128]{2,0,1:T(8,128)S(1)} %fusion.34, ...), kind=kOutput, calls=%fused_computation.44 | convolution fusion | flops 406847360 | bytes 13648384 | tf_op jit(solution)/shard_map/pij,pjr->pir/dot_general | solution.py:100
  460.2 47.3 %psum.22 = f32[128]{0:T(128)S(1)} all-reduce(f32[128]{0:T(128)S(1)} %get-tuple-element.18), channel_id=1, replica_groups=mesh['sector'=4,'axial'=8] {'sector','axial'}, use_global_device_ids=true, to_apply=%region_13.14 | all-reduce | flops 128 | bytes 1024 | tf_op jit(solution)/shard_map/psum | solution.py:119
  507.6 3.5 multiply_reduce_fusion.1
  511.1 28.6 %all-gather.5 = f32[32,1,128]{2,1,0:T(1,128)S(1)} all-gather(f32[1,1,128]{2,1,0:T(1,128)S(1)} %bitcast.92), channel_id=4, replica_groups=mesh['sector'=4,'axial'=8] {'sector','axial'}, dimensions={0}, use_global_device_ids=true | all-gather | bytes 16896 | tf_op jit(solution)/shard_map/all_gather | solution.py:87
  539.8 3.6 multiply_add_fusion.1
  543.4 3.0 gather_fusion.12
  546.3 4.8 collective-permute-start.14
  551.1 3.0 gather_fusion.10
  554.1 6.9 %collective-permute-start.12 = (f32[16,64,128]{2,1,0:T(8,128)}, f32[16,64,128]{2,1,0:T(8,128)}, u32[]{:S(2)}, u32[]{:S(2)}) collective-permute-start(f32[16,64,128]{2,1,0:T(8,128)} %gather_fusion.10), channel_id=1, source_target_pairs={{0,24},{8,0},{16,8},{24,16},{1,25},{9,1},{17,9},{25,17},{2,26},{10... | collective-permute-start | bytes 1572872 | tf_op jit(solution)/shard_map/ppermute | solution.py:12
  573.4 3.6 collective-permute-done.15
  578.2 5.0 collective-permute-done.13
  584.4 13.9 %multiply_reduce_fusion = (f32[128]{0:T(128)S(1)}, f32[64,64,128]{2,1,0:T(8,128)}) fusion(f32[64,64,128]{2,1,0:T(8,128)S(1)} %copy-done.5, f32[64,64,128]{2,0,1:T(8,128)S(1)} %fusion.20, f32[64,64,128]{2,0,1:T(8,128)S(1)} %fusion.22, f32[64,64,128]{2,0,1:T(8,128)S(1)} %fusion.24, f32[64,64,128]{2,0,1:T(8,128)S(1)} %fusion.26, ...), kind=kOutput, calls=%fused_computation.40 | convolution fusion | flops 406847360 | bytes 13648384 | tf_op jit(solution)/shard_map/pij,pjr->pir/dot_general | solution.py:100
  598.2 47.1 %psum.23 = f32[128]{0:T(128)S(1)} all-reduce(f32[128]{0:T(128)S(1)} %get-tuple-element.20), channel_id=1, replica_groups=mesh['sector'=4,'axial'=8] {'sector','axial'}, use_global_device_ids=true, to_apply=%region_17.18 | all-reduce | flops 128 | bytes 1024 | tf_op jit(solution)/shard_map/psum | solution.py:119
  645.4 5.3 multiply_subtract_fusion
  (118 shorter events, 73.4 us)
Async XLA Ops:
  5.4 11.0 %all-to-all-start.1 = ((s32[32,8,1]{1,2,0:T(1,128)}), s32[32,8,1]{1,2,0:T(1,128)S(1)}, u32[]{:S(2)}, u32[]{:S(2)}) async-start(s32[32,8,1]{1,2,0:T(1,128)} %bitcast.5), calls=%async_computation.1 | async-start | bytes 32768 | tf_op jit(solution)/shard_map/all_to_all | solution.py:55
  16.4 12.0 %all-to-all-start = ((s32[32,8,1]{1,2,0:T(1,128)}), s32[32,8,1]{1,2,0:T(1,128)S(1)}, u32[]{:S(2)}, u32[]{:S(2)}) async-start(s32[32,8,1]{1,2,0:T(1,128)} %bitcast.3), calls=%async_computation | async-start | bytes 32768 | tf_op jit(solution)/shard_map/all_to_all | solution.py:54
  21.0 5.6 copy-start.8
  28.3 47.2 %all-to-all-start.2 = ((s32[32,1,512]{2,1,0:T(1,128)}), s32[32,1,512]{2,1,0:T(1,128)S(1)}, u32[]{:S(2)}, u32[]{:S(2)}) async-start(s32[32,1,512]{2,1,0:T(1,128)} %reshape.310), calls=%async_computation.2 | async-start | bytes 131072 | tf_op jit(solution)/shard_map/all_to_all | solution.py:53
  75.5 5.9 copy-start.7
  75.5 7.5 %copy-start.10 = (s32[2,16,2]{1,2,0:T(2,128)S(1)}, s32[2,16,2]{1,2,0:T(2,128)}, u32[]{:S(2)}) copy-start(s32[2,16,2]{1,2,0:T(2,128)} %param.17) | copy-start | bytes 772
  75.5 14.8 %copy-start.9 = (f32[4096]{0:T(1024)S(1)}, f32[4096]{0:T(1024)}, u32[]{:S(2)}) copy-start(f32[4096]{0:T(1024)} %param.16) | copy-start | bytes 49156
  75.6 96.7 %all-to-all-start.3 = ((f32[32,1,32768]{2,1,0:T(1,128)}), f32[32,1,32768]{2,1,0:T(1,128)}, u32[]{:S(2)}, u32[]{:S(2)}) async-start(f32[32,1,32768]{2,1,0:T(1,128)} %reshape.308), calls=%async_computation.3 | async-start | bytes 8388608 | tf_op jit(solution)/shard_map/all_to_all | solution.py:52
  81.5 148.4 %collective-permute-start.1 = (f32[16,64]{1,0:T(8,128)S(1)}, f32[16,64]{1,0:T(8,128)S(1)}, u32[]{:S(2)}, u32[]{:S(2)}) collective-permute-start(f32[16,64]{1,0:T(8,128)S(1)} %get-tuple-element.7), channel_id=1, source_target_pairs={{0,8},{8,16},{16,24},{24,0},{1,9},{9,17},{17,25},{25,1},{2,10},{10... | collective-permute-start | bytes 12296 | tf_op jit(solution)/shard_map/ppermute | solution.py:12
  83.0 146.8 %collective-permute-start = (s32[16]{0:T(128)S(1)}, s32[16]{0:T(128)S(1)}, u32[]{:S(2)}, u32[]{:S(2)}) collective-permute-start(s32[16]{0:T(128)S(1)} %get-tuple-element.11), channel_id=1, source_target_pairs={{0,8},{8,16},{16,24},{24,0},{1,9},{9,17},{17,25},{25,1},{2,10},{10... | collective-permute-start | bytes 200 | tf_op jit(solution)/shard_map/ppermute | solution.py:12
  84.6 145.6 %collective-permute-start.3 = (f32[16,64]{1,0:T(8,128)S(1)}, f32[16,64]{1,0:T(8,128)S(1)}, u32[]{:S(2)}, u32[]{:S(2)}) collective-permute-start(f32[16,64]{1,0:T(8,128)S(1)} %get-tuple-element.6), channel_id=1, source_target_pairs={{0,1},{1,2},{2,3},{3,4},{4,5},{5,6},{6,7},{8,9},{9,10},{10,11},{11... | collective-permute-start | bytes 12296 | tf_op jit(solution)/shard_map/ppermute | solution.py:18
  86.5 17.3 %collective-permute-start.2 = (s32[16]{0:T(128)S(1)}, s32[16]{0:T(128)S(1)}, u32[]{:S(2)}, u32[]{:S(2)}) collective-permute-start(s32[16]{0:T(128)S(1)} %get-tuple-element.10), channel_id=1, source_target_pairs={{0,1},{1,2},{2,3},{3,4},{4,5},{5,6},{6,7},{8,9},{9,10},{10,11},{11... | collective-permute-start | bytes 200 | tf_op jit(solution)/shard_map/ppermute | solution.py:18
  224.9 5.6 copy-start
  235.1 52.6 %collective-permute-start.6 = (f32[16,64,128]{2,1,0:T(8,128)}, f32[16,64,128]{2,1,0:T(8,128)}, u32[]{:S(2)}, u32[]{:S(2)}) collective-permute-start(f32[16,64,128]{2,1,0:T(8,128)} %gather_fusion.4), channel_id=1, source_target_pairs={{1,0},{2,1},{3,2},{4,3},{5,4},{6,5},{7,6},{9,8},{10,9},{11,10},{12... | collective-permute-start | bytes 1572872 | tf_op jit(solution)/shard_map/ppermute | solution.py:18
  245.4 45.9 %collective-permute-start.4 = (f32[16,64,128]{2,1,0:T(8,128)}, f32[16,64,128]{2,1,0:T(8,128)}, u32[]{:S(2)}, u32[]{:S(2)}) collective-permute-start(f32[16,64,128]{2,1,0:T(8,128)} %gather_fusion.2), channel_id=1, source_target_pairs={{0,24},{8,0},{16,8},{24,16},{1,25},{9,1},{17,9},{25,17},{2,26},{10... | collective-permute-start | bytes 1572872 | tf_op jit(solution)/shard_map/ppermute | solution.py:12
  289.0 10.8 %collective-permute-start.7 = (f32[16,64,128]{2,1,0:T(8,128)S(1)}, f32[16,64,128]{2,1,0:T(8,128)S(1)}, u32[]{:S(2)}, u32[]{:S(2)}) collective-permute-start(f32[16,64,128]{2,1,0:T(8,128)S(1)} %subtract_multiply_fusion.4), channel_id=1, source_target_pairs={{0,1},{1,2},{2,3},{3,4},{4,5},{5,6},{6,7},{8,9},{9,10},{10,11},{11... | collective-permute-start | bytes 1572872 | tf_op jit(solution)/shard_map/ppermute | solution.py:18
  292.5 18.2 %collective-permute-start.5 = (f32[16,64,128]{2,1,0:T(8,128)S(1)}, f32[16,64,128]{2,1,0:T(8,128)S(1)}, u32[]{:S(2)}, u32[]{:S(2)}) collective-permute-start(f32[16,64,128]{2,1,0:T(8,128)S(1)} %subtract_multiply_fusion.5), channel_id=1, source_target_pairs={{0,8},{8,16},{16,24},{24,0},{1,9},{9,17},{17,25},{25,1},{2,10},{10... | collective-permute-start | bytes 1572872 | tf_op jit(solution)/shard_map/ppermute | solution.py:12
  295.4 16.5 %copy-start.2 = (f32[64,64,64]{2,0,1:T(8,128)S(1)}, f32[64,64,64]{2,0,1:T(8,128)}, u32[]{:S(2)}) copy-start(f32[64,64,64]{2,0,1:T(8,128)} %fusion) | copy-start | bytes 3145732
  295.4 16.5 %copy-start.6 = (f32[64,64,128]{2,1,0:T(8,128)S(1)}, f32[64,64,128]{2,1,0:T(8,128)}, u32[]{:S(2)}) copy-start(f32[64,64,128]{2,1,0:T(8,128)} %broadcast_divide_fusion) | copy-start | bytes 6291460
  408.3 18.9 %collective-permute-start.10 = (f32[16,64,128]{2,1,0:T(8,128)}, f32[16,64,128]{2,1,0:T(8,128)}, u32[]{:S(2)}, u32[]{:S(2)}) collective-permute-start(f32[16,64,128]{2,1,0:T(8,128)} %gather_fusion.8), channel_id=1, source_target_pairs={{1,0},{2,1},{3,2},{4,3},{5,4},{6,5},{7,6},{9,8},{10,9},{11,10},{12... | collective-permute-start | bytes 1572872 | tf_op jit(solution)/shard_map/ppermute | solution.py:18
  416.1 15.7 %collective-permute-start.8 = (f32[16,64,128]{2,1,0:T(8,128)}, f32[16,64,128]{2,1,0:T(8,128)}, u32[]{:S(2)}, u32[]{:S(2)}) collective-permute-start(f32[16,64,128]{2,1,0:T(8,128)} %gather_fusion.6), channel_id=1, source_target_pairs={{0,24},{8,0},{16,8},{24,16},{1,25},{9,1},{17,9},{25,17},{2,26},{10... | collective-permute-start | bytes 1572872 | tf_op jit(solution)/shard_map/ppermute | solution.py:12
  428.5 10.5 %collective-permute-start.11 = (f32[16,64,128]{2,1,0:T(8,128)S(1)}, f32[16,64,128]{2,1,0:T(8,128)S(1)}, u32[]{:S(2)}, u32[]{:S(2)}) collective-permute-start(f32[16,64,128]{2,1,0:T(8,128)S(1)} %subtract_multiply_fusion.2), channel_id=1, source_target_pairs={{0,1},{1,2},{2,3},{3,4},{4,5},{5,6},{6,7},{8,9},{9,10},{10,11},{11... | collective-permute-start | bytes 1572872 | tf_op jit(solution)/shard_map/ppermute | solution.py:18
  433.0 12.2 %collective-permute-start.9 = (f32[16,64,128]{2,1,0:T(8,128)S(1)}, f32[16,64,128]{2,1,0:T(8,128)S(1)}, u32[]{:S(2)}, u32[]{:S(2)}) collective-permute-start(f32[16,64,128]{2,1,0:T(8,128)S(1)} %subtract_multiply_fusion.3), channel_id=1, source_target_pairs={{0,8},{8,16},{16,24},{24,0},{1,9},{9,17},{17,25},{25,1},{2,10},{10... | collective-permute-start | bytes 1572872 | tf_op jit(solution)/shard_map/ppermute | solution.py:12
  435.4 11.0 %copy-start.1 = (f32[64,64,128]{2,1,0:T(8,128)S(1)}, f32[64,64,128]{2,1,0:T(8,128)}, u32[]{:S(2)}) copy-start(f32[64,64,128]{2,1,0:T(8,128)} %multiply_add_fusion.2) | copy-start | bytes 6291460
  435.4 11.0 %copy-start.3 = (f32[64,64,64]{2,0,1:T(8,128)S(1)}, f32[64,64,64]{2,0,1:T(8,128)}, u32[]{:S(2)}) copy-start(f32[64,64,64]{2,0,1:T(8,128)} %fusion) | copy-start | bytes 3145732
  546.3 19.0 %collective-permute-start.14 = (f32[16,64,128]{2,1,0:T(8,128)}, f32[16,64,128]{2,1,0:T(8,128)}, u32[]{:S(2)}, u32[]{:S(2)}) collective-permute-start(f32[16,64,128]{2,1,0:T(8,128)} %gather_fusion.12), channel_id=1, source_target_pairs={{1,0},{2,1},{3,2},{4,3},{5,4},{6,5},{7,6},{9,8},{10,9},{11,10},{12... | collective-permute-start | bytes 1572872 | tf_op jit(solution)/shard_map/ppermute | solution.py:18
  554.1 15.7 %collective-permute-start.12 = (f32[16,64,128]{2,1,0:T(8,128)}, f32[16,64,128]{2,1,0:T(8,128)}, u32[]{:S(2)}, u32[]{:S(2)}) collective-permute-start(f32[16,64,128]{2,1,0:T(8,128)} %gather_fusion.10), channel_id=1, source_target_pairs={{0,24},{8,0},{16,8},{24,16},{1,25},{9,1},{17,9},{25,17},{2,26},{10... | collective-permute-start | bytes 1572872 | tf_op jit(solution)/shard_map/ppermute | solution.py:12
  566.5 10.5 %collective-permute-start.15 = (f32[16,64,128]{2,1,0:T(8,128)S(1)}, f32[16,64,128]{2,1,0:T(8,128)S(1)}, u32[]{:S(2)}, u32[]{:S(2)}) collective-permute-start(f32[16,64,128]{2,1,0:T(8,128)S(1)} %subtract_multiply_fusion), channel_id=1, source_target_pairs={{0,1},{1,2},{2,3},{3,4},{4,5},{5,6},{6,7},{8,9},{9,10},{10,11},{11... | collective-permute-start | bytes 1572872 | tf_op jit(solution)/shard_map/ppermute | solution.py:18
  571.0 12.2 %collective-permute-start.13 = (f32[16,64,128]{2,1,0:T(8,128)S(1)}, f32[16,64,128]{2,1,0:T(8,128)S(1)}, u32[]{:S(2)}, u32[]{:S(2)}) collective-permute-start(f32[16,64,128]{2,1,0:T(8,128)S(1)} %subtract_multiply_fusion.1), channel_id=1, source_target_pairs={{0,8},{8,16},{16,24},{24,0},{1,9},{9,17},{17,25},{25,1},{2,10},{10... | collective-permute-start | bytes 1572872 | tf_op jit(solution)/shard_map/ppermute | solution.py:12
  573.4 11.0 %copy-start.4 = (f32[64,64,64]{2,0,1:T(8,128)S(1)}, f32[64,64,64]{2,0,1:T(8,128)}, u32[]{:S(2)}) copy-start(f32[64,64,64]{2,0,1:T(8,128)} %fusion) | copy-start | bytes 3145732
  573.4 11.0 %copy-start.5 = (f32[64,64,128]{2,1,0:T(8,128)S(1)}, f32[64,64,128]{2,1,0:T(8,128)}, u32[]{:S(2)}) copy-start(f32[64,64,128]{2,1,0:T(8,128)} %multiply_add_fusion.1) | copy-start | bytes 6291460
